TPU v7x, 32 devices: a whole 2x2x4 slice. The times are simulated.
32 devices in a mesh: row: 4 (over z), col: 4 (over x, core), layer: 2 (over y).
Axes of the slice: x: 2, y: 2, z: 4, core: 2. Of those that a mesh axis runs over, the one named last changes fastest.
Arguments:
- intersection: bfloat16 [2048, 2, 1024], P('row', 'layer', 'col'), may hold values from -6 to 6
- density: bfloat16 [2, 1024, 2, 1024], P('layer', 'row', None, 'col'), may hold values from -0.125 to 0.125
- hamiltonian: bfloat16 [2, 1024, 2, 1024], P('layer', 'row', None, 'col'), may hold values from -0.125 to 0.125
- intersection_pattern: int32 [16, 2, 8], P('row', 'layer', 'col'), may hold values 0 or 1
- density_pattern: int32 [2, 8, 2, 8], P('layer', 'row', None, 'col'), may hold values 0 or 1
- hamiltonian_pattern: int32 [2, 8, 2, 8], P('layer', 'row', None, 'col'), may hold values 0 or 1
- product_filter: int32 [16, 2, 8], P('row', 'layer', 'col'), may hold values 0 or 1
Outputs:
- gradient_term: bfloat16 [2048, 2, 1024], P('row', 'layer', 'col')
All inputs are finite; a program needn't handle non-finite values. No bound on the sum of `intersection_pattern` or of `density_pattern` or of `hamiltonian_pattern` or of `product_filter` on one device may be relied on, other than what follows from the above.
Results may differ from a plain program's by a relative error of at most 0.005.
Values may be sent and summed in bfloat16 or wider, within the bound.
No kernel may reach another device: no remote copies, remote signals or barrier semaphores. Data moves between devices by JAX's collectives and lax.ppermute only.
A program may use at most 64 MiB of HBM per device.

v0:
```python
import jax
import jax.numpy as jnp
from jax import lax
from jax.sharding import PartitionSpec as P


def mask_left(block_tile, pattern):
    row_count, _, col_count = block_tile.shape
    row_blocks = pattern.shape[0]
    col_blocks = pattern.shape[2]
    blocks = block_tile.reshape(
        row_blocks, row_count // row_blocks, col_blocks, col_count // col_blocks
    )
    blocks = blocks * pattern.reshape(row_blocks, 1, col_blocks, 1).astype(jnp.bfloat16)
    return blocks.reshape(row_count, col_count)


def mask_right(block_tile, pattern):
    _, row_count, layers, col_count = block_tile.shape
    row_blocks = pattern.shape[1]
    col_blocks = pattern.shape[3]
    blocks = block_tile.reshape(
        row_blocks, row_count // row_blocks, layers, col_blocks, col_count // col_blocks
    )
    blocks = blocks * pattern.reshape(row_blocks, 1, layers, col_blocks, 1).astype(jnp.bfloat16)
    return blocks.reshape(row_count, layers * col_count)


def multiply(left_tile, right_tile):
    whole_left = lax.all_gather(left_tile, "col", axis=1, tiled=True)
    row_count = whole_left.shape[0]
    layers = lax.axis_size("layer")
    column_span = right_tile.shape[1] // layers
    partial_value = jnp.dot(
        whole_left,
        lax.all_gather(right_tile, "row", axis=0, tiled=True),
        preferred_element_type=jnp.float32,
    )
    return lax.psum_scatter(
        partial_value.reshape(row_count, layers, column_span),
        "layer",
        scatter_dimension=1,
        tiled=True,
    )


def local(
    intersection,
    density,
    hamiltonian,
    intersection_pattern,
    density_pattern,
    hamiltonian_pattern,
    product_filter,
):
    left_factor = mask_left(intersection, intersection_pattern)
    right_factor = mask_right(density, density_pattern)
    raw_product = multiply(left_factor, right_factor)
    filtered = mask_left(raw_product.astype(jnp.bfloat16), product_filter)
    masked_ham = mask_right(hamiltonian, hamiltonian_pattern)
    return multiply(filtered, masked_ham).astype(jnp.bfloat16)


def solution(mesh):
    placed = (
        P("row", "layer", "col"),
        P("layer", "row", None, "col"),
        P("layer", "row", None, "col"),
        P("row", "layer", "col"),
        P("layer", "row", None, "col"),
        P("layer", "row", None, "col"),
        P("row", "layer", "col"),
    )
    return jax.shard_map(
        local, mesh=mesh, in_specs=placed, out_specs=P("row", "layer", "col"), check_vma=False
    )
```

profile of v0, /device:TPU:0, one launch (start us, length us, event | category | flops | bytes accessed | tf_op | source)
XLA Modules:
  0.0 161.6 jit_solution(11556054652740069047)
XLA Ops:
  6.5 0.0 all-gather.7.cloned.1.call-start
  6.5 0.7 convert_bitcast_fusion.1
  7.2 0.2 mul.47
  7.4 0.0 copy-start.1
  7.4 0.1 mul.48
  7.6 0.8 copy-done.1
  8.4 0.0 copy-start.4
  8.4 0.8 mul.49
  9.2 0.0 copy-start
  9.2 0.0 all-gather.7.cloned.1.call-update
  9.2 0.0 all-gather.5.cloned.1.call-start
  9.3 0.0 copy-done.4
  9.3 0.1 copy.8
  9.4 0.2 mul.44
  9.6 0.5 copy-done
  10.2 0.7 bitcast_multiply_fusion.1
  10.9 0.0 all-gather.5.cloned.1.call-update
  10.9 0.0 reduce-scatter.3.cloned.1.call-start
  11.0 29.0 %all-gather.7.cloned.1.call-done = bf16[1024,512]{1,0:T(8,128)(2,1)} async-done(((bf16[256,512]{1,0:T(8,128)(2,1)}), bf16[1024,512]{1,0:T(8,128)(2,1)}) %all-gather.7.cloned.1.call-update) | async-done | bytes 1048592 | tf_op jit(solution)/shard_map/all_gather | solution.py:36
  40.0 17.9 %all-gather.5.cloned.1.call-done = bf16[512,1024]{1,0:T(8,128)(2,1)} async-done(((bf16[512,256]{1,0:T(8,128)(2,1)}), bf16[512,1024]{1,0:T(8,128)(2,1)}) %all-gather.5.cloned.1.call-update) | async-done | bytes 1048592 | tf_op jit(solution)/shard_map/all_gather | solution.py:30
  57.9 3.3 %fusion = f32[512,512]{0,1:T(8,128)} fusion(bf16[512,1024]{1,0:T(8,128)(2,1)} %all-gather.5.cloned.1.call-done, bf16[1024,512]{1,0:T(8,128)(2,1)} %all-gather.7.cloned.1.call-done), kind=kOutput, calls=%fused_computation.6 | convolution fusion | flops 536870912 | bytes 3145728 | tf_op jit(solution)/shard_map/dot_general | solution.py:34
  61.2 0.0 copy-start.3
  61.2 0.0 reduce-scatter.3.cloned.1.call-update
  61.2 0.0 all-gather.11.cloned.1.call-start
  61.3 0.6 copy-done.3
  61.9 0.2 mul.53
  62.1 0.0 copy-start.2
  62.1 0.1 mul.54
  62.2 0.8 copy-done.2
  63.1 0.8 mul.55
  63.9 0.0 copy-start.5
  63.9 0.0 all-gather.11.cloned.1.call-update
  63.9 0.0 all-gather.9.cloned.1.call-start
  64.0 0.6 copy-done.5
  64.6 17.1 %reduce-scatter.3.cloned.1.call-done = f32[512,1,256]{0,2,1:T(8,128)} async-done(((f32[512,2,256]{0,2,1:T(8,128)}), f32[512,1,256]{0,2,1:T(8,128)}) %reduce-scatter.3.cloned.1.call-update) | async-done | bytes 524304 | tf_op jit(solution)/shard_map/reduce_scatter | solution.py:39
  81.7 0.1 mul.50
  81.9 1.8 %bitcast_multiply_fusion = bf16[512,256]{0,1:T(8,128)(2,1)} fusion(bf16[32,8,4,128]{3,2,1,0:T(4,128)(2,1)S(1)} %bitcast.39, f32[512,1,256]{0,2,1:T(8,128)} %reduce-scatter.3.cloned.1.call-done), kind=kLoop, calls=%fused_computation | loop fusion | flops 262144 | bytes 1048576 | tf_op jit(solution)/shard_map/mul | solution.py:14
  83.7 0.0 all-gather.9.cloned.1.call-update
  83.7 0.0 reduce-scatter.5.cloned.1.call-start
  83.7 27.4 %all-gather.11.cloned.1.call-done = bf16[1024,512]{1,0:T(8,128)(2,1)} async-done(((bf16[256,512]{1,0:T(8,128)(2,1)}), bf16[1024,512]{1,0:T(8,128)(2,1)}) %all-gather.11.cloned.1.call-update) | async-done | bytes 1048592 | tf_op jit(solution)/shard_map/all_gather | solution.py:36
  111.2 17.7 %all-gather.9.cloned.1.call-done = bf16[512,1024]{0,1:T(8,128)(2,1)} async-done(((bf16[512,256]{0,1:T(8,128)(2,1)}), bf16[512,1024]{0,1:T(8,128)(2,1)}) %all-gather.9.cloned.1.call-update) | async-done | bytes 1048592 | tf_op jit(solution)/shard_map/all_gather | solution.py:30
  128.9 2.3 %fusion.1 = f32[512,512]{0,1:T(8,128)S(1)} fusion(bf16[512,1024]{0,1:T(8,128)(2,1)} %all-gather.9.cloned.1.call-done, bf16[1024,512]{1,0:T(8,128)(2,1)} %all-gather.11.cloned.1.call-done), kind=kOutput, calls=%fused_computation.7 | convolution fusion | flops 536870912 | bytes 3145728 | tf_op jit(solution)/shard_map/dot_general | solution.py:34
  131.2 1.3 copy.9
  132.5 0.0 reduce-scatter.5.cloned.1.call-update
  132.5 20.5 %reduce-scatter.5.cloned.1.call-done = f32[512,1,256]{2,0,1:T(8,128)} async-done(((f32[512,2,256]{2,0,1:T(8,128)}), f32[512,1,256]{2,0,1:T(8,128)}) %reduce-scatter.5.cloned.1.call-update) | async-done | bytes 524304 | tf_op jit(solution)/shard_map/reduce_scatter | solution.py:39
  153.0 1.8 %convert_element_type.59 = bf16[512,1,256]{2,0,1:T(8,128)(2,1)} convert(f32[512,1,256]{2,0,1:T(8,128)} %reduce-scatter.5.cloned.1.call-done) | non-fusion elementwise | flops 131072 | bytes 786432 | tf_op jit(solution)/shard_map/convert_element_type | solution.py:61
  (5 shorter events, 0.1 us)
Async XLA Ops:
  6.5 33.5 %all-gather.7.cloned.1.call-start = ((), (), s32[]{:S(2)}) async-start(), calls=%async_computation.3 | async-start | bytes 1310720 | tf_op jit(solution)/shard_map/all_gather | solution.py:36
  7.4 1.0 copy-start.1
  8.4 0.9 copy-start.4
  9.2 0.9 copy-start
  9.2 48.7 %all-gather.5.cloned.1.call-start = ((), (), s32[]{:S(2)}) async-start(), calls=%async_computation.2 | async-start | bytes 1310720 | tf_op jit(solution)/shard_map/all_gather | solution.py:30
  10.9 70.8 %reduce-scatter.3.cloned.1.call-start = ((), (), s32[]{:S(2)}) async-start(), calls=%async_computation.4 | async-start | bytes 1572864 | tf_op jit(solution)/shard_map/reduce_scatter | solution.py:39
  61.2 0.7 copy-start.3
  61.2 49.9 %all-gather.11.cloned.1.call-start = ((), (), s32[]{:S(2)}) async-start(), calls=%async_computation.6 | async-start | bytes 1310720 | tf_op jit(solution)/shard_map/all_gather | solution.py:36
  62.1 1.0 copy-start.2
  63.9 0.7 copy-start.5
  63.9 65.0 %all-gather.9.cloned.1.call-start = ((), (), s32[]{:S(2)}) async-start(), calls=%async_computation.5 | async-start | bytes 1310720 | tf_op jit(solution)/shard_map/all_gather | solution.py:30
  83.7 69.3 %reduce-scatter.5.cloned.1.call-start = ((), (), s32[]{:S(2)}) async-start(), calls=%async_computation.7 | async-start | bytes 1572864 | tf_op jit(solution)/shard_map/reduce_scatter | solution.py:39
Sparse Core Ops, SparseCore 0:
  9.4 30.6 all-gather.6
  41.6 16.3 all-gather.4
  61.4 20.3 reduce-scatter.2
  83.2 27.9 all-gather.10
  112.7 16.2 all-gather.8
  132.7 20.3 reduce-scatter.4
where the time goes:
time: 162 us
  waiting for transfers between devices  130 us (80%)
  between operations  13.6 us (8%)
  other arithmetic  6.58 us (4%)
  local copies, waits for them, and re-layouts  5.88 us (4%)
  matrix products  5.57 us (3%)
    all_gather x2, waiting for transfers between devices, multiply(): lax.all_gather(right_tile, 'row', axis=0, tiled=True)  56.5 us
    reduce_scatter x2, waiting for transfers between devices, multiply(): lax.psum_scatter(partial_value.reshape(row_count, layers, column_span), '...  37.6 us
    all_gather x2, waiting for transfers between devices, multiply(): whole_left = lax.all_gather(left_tile, 'col', axis=1, tiled=True)  35.6 us
    dot_general x2, matrix products, multiply(): jnp.dot(whole_left, lax.all_gather(right_tile, 'row', axis=0, tiled=True)...  5.57 us
    unnamed x14, local copies, waits for them, and re-layouts  3.49 us
  transfers between devices with their start and end apart: 6, of which 6 were waited for; matrix products, arithmetic and copies ran while one was open for 3% of the time, Pallas kernels for 0%

commit v1 on v0

--- a/solution.py
+++ b/solution.py
@@ -2,6 +2,17 @@
 import jax.numpy as jnp
 from jax import lax
 from jax.sharding import PartitionSpec as P
+
+
+def turned_line(block, mesh_axis, dim):
+    size = lax.axis_size(mesh_axis)
+    forward = [(i, (i + 1) % size) for i in range(size)]
+    parts = [block]
+    for reach in range(1, size):
+        parts = [lax.ppermute(parts[0], mesh_axis, forward), *parts]
+    whole = jnp.concatenate(parts, axis=dim)
+    places = (lax.axis_index(mesh_axis) + 1) * parts[-1].shape[dim]
+    return jnp.roll(whole, places, axis=dim)
 
 
 def mask_left(block_tile, pattern):
@@ -27,7 +38,7 @@
 
 
 def multiply(left_tile, right_tile):
-    whole_left = lax.all_gather(left_tile, "col", axis=1, tiled=True)
+    whole_left = turned_line(left_tile, "col", 1)
     row_count = whole_left.shape[0]
     layers = lax.axis_size("layer")
     column_span = right_tile.shape[1] // layers

time: 162 us -> 129 us (0.80)
  waiting for transfers between devices: 130 us -> 96.2 us
  matrix products: 5.57 us -> 9.07 us
  local copies, waits for them, and re-layouts: 5.88 us -> 4.08 us
    all_gather x2 -> x0, waiting for transfers between devices: 35.6 us -> none  [multiply(): whole_left = lax.all_gather(left_tile, 'col', axis=1, tiled=True)]
    ppermute x0 -> x6, waiting for transfers between devices: none -> 29.2 us  [turned_line(): parts = [lax.ppermute(parts[0], mesh_axis, forward), *parts]]
    all_gather x2, waiting for transfers between devices: 56.5 us -> 29 us  [multiply(): lax.all_gather(right_tile, 'row', axis=0, tiled=True)]
    dot_general x2, matrix products: 5.57 us -> 9.07 us  [multiply(): jnp.dot(whole_left, lax.all_gather(right_tile, 'row', axis=0, tiled=True)...]
    unnamed x14 -> x12, local copies, waits for them, and re-layouts: 3.49 us -> 1.68 us
  transfers between devices with their start and end apart: 6 -> 10, of which waited for: 6 -> 9; matrix products, arithmetic and copies ran while one was open for 3% -> 2% of each run, Pallas kernels for 0% -> 0%
where the time goes in v1:
time: 129 us; the launch traced here: 128 us
  waiting for transfers between devices  96.2 us (75%)
  between operations  13.3 us (10%)
  matrix products  9.07 us (7%)
  other arithmetic  5.16 us (4%)
  local copies, waits for them, and re-layouts  4.08 us (3%)
    reduce_scatter x2, waiting for transfers between devices, multiply(): lax.psum_scatter(partial_value.reshape(row_count, layers, column_span), '...  38 us
    ppermute x6, waiting for transfers between devices, turned_line(): parts = [lax.ppermute(parts[0], mesh_axis, forward), *parts]  29.2 us
    all_gather x2, waiting for transfers between devices, multiply(): lax.all_gather(right_tile, 'row', axis=0, tiled=True)  29 us
    dot_general x2, matrix products, multiply(): jnp.dot(whole_left, lax.all_gather(right_tile, 'row', axis=0, tiled=True)...  9.07 us
  transfers between devices with their start and end apart: 10, of which 9 were waited for; matrix products, arithmetic and copies ran while one was open for 2% of the time, Pallas kernels for 0%

profile of v1, /device:TPU:0, one launch (start us, length us, event | category | flops | bytes accessed | tf_op | source)
XLA Modules:
  0.0 128.5 jit_solution(15443183676825115928)
XLA Ops:
  6.5 0.0 all-gather.3.cloned.1.call-start
  6.5 0.7 convert_bitcast_fusion.1
  7.2 0.2 mul.52
  7.4 0.0 copy-start.3
  7.4 0.1 mul.53
  7.6 0.0 copy-start
  7.6 1.0 copy.11
  8.6 0.8 mul.54
  9.4 0.0 all-gather.3.cloned.1.call-update
  9.4 0.0 reduce-scatter.3.cloned.1.call-start
  9.4 0.0 copy-done.3
  9.5 0.1 copy.8
  9.6 0.2 mul.48
  9.8 0.0 copy-done
  9.8 0.5 collective-permute-start
  10.3 6.0 %collective-permute-done = bf16[512,256]{1,0:T(8,128)(2,1)S(1)} collective-permute-done((bf16[512,256]{1,0:T(8,128)(2,1)S(1)}, bf16[512,256]{1,0:T(8,128)(2,1)S(1)}, u32[]{:S(2)}, u32[]{:S(2)}) %collective-permute-start) | collective-permute-done | bytes 262176 | tf_op jit(solution)/shard_map/ppermute | solution.py:12
  16.3 0.0 collective-permute-start.1
  16.3 5.8 %collective-permute-done.1 = bf16[512,256]{1,0:T(8,128)(2,1)S(1)} collective-permute-done((bf16[512,256]{1,0:T(8,128)(2,1)S(1)}, bf16[512,256]{1,0:T(8,128)(2,1)S(1)}, u32[]{:S(2)}, u32[]{:S(2)}) %collective-permute-start.1) | collective-permute-done | bytes 262176 | tf_op jit(solution)/shard_map/ppermute | solution.py:12
  22.1 0.0 collective-permute-start.2
  22.1 5.8 %collective-permute-done.2 = bf16[512,256]{1,0:T(8,128)(2,1)S(1)} collective-permute-done((bf16[512,256]{1,0:T(8,128)(2,1)S(1)}, bf16[512,256]{1,0:T(8,128)(2,1)S(1)}, u32[]{:S(2)}, u32[]{:S(2)}) %collective-permute-start.2) | collective-permute-done | bytes 262176 | tf_op jit(solution)/shard_map/ppermute | solution.py:12
  27.9 12.3 %all-gather.3.cloned.1.call-done = bf16[1024,512]{1,0:T(8,128)(2,1)} async-done(((bf16[256,512]{1,0:T(8,128)(2,1)}), bf16[1024,512]{1,0:T(8,128)(2,1)}) %all-gather.3.cloned.1.call-update) | async-done | bytes 1048592 | tf_op jit(solution)/shard_map/all_gather | solution.py:47
  40.2 4.1 %fusion.14 = f32[512,512]{0,1:T(8,128)} fusion(bf16[1024,512]{1,0:T(8,128)(2,1)} %all-gather.3.cloned.1.call-done, s32[]{:T(128)S(6)} %select_n.13, bf16[512,256]{1,0:T(8,128)(2,1)S(1)} %collective-permute-done.2, bf16[512,256]{1,0:T(8,128)(2,1)S(1)} %collective-permute-done.1, bf16[512,256]{1,0:T(8,128)(2,1)S(1)} %collective-permute-done, ...), kind=kOutput, calls=%fused_computation.28 | convolution fusion | flops 545259520 | bytes 3145732 | tf_op jit(solution)/shard_map/dot_general | solution.py:45
  44.2 0.0 copy-start.2
  44.2 0.0 copy-start.1
  44.2 0.0 reduce-scatter.3.cloned.1.call-update
  44.3 0.0 all-gather.5.cloned.1.call-start
  44.3 0.6 copy-done.2
  44.9 0.2 mul.58
  45.1 0.0 copy-start.4
  45.1 0.1 mul.59
  45.2 0.0 copy-done.1
  45.3 0.8 mul.60
  46.1 0.0 all-gather.5.cloned.1.call-update
  46.1 0.0 reduce-scatter.5.cloned.1.call-start
  46.1 0.0 copy-done.4
  46.2 18.0 %reduce-scatter.3.cloned.1.call-done = f32[512,1,256]{0,2,1:T(8,128)} async-done(((f32[512,2,256]{0,2,1:T(8,128)}), f32[512,1,256]{0,2,1:T(8,128)}) %reduce-scatter.3.cloned.1.call-update) | async-done | bytes 524304 | tf_op jit(solution)/shard_map/reduce_scatter | solution.py:50
  64.2 0.1 mul.55
  64.3 1.1 bitcast_multiply_fusion
  65.5 0.1 collective-permute-start.3
  65.5 5.8 %collective-permute-done.3 = bf16[512,256]{0,1:T(8,128)(2,1)S(1)} collective-permute-done((bf16[512,256]{0,1:T(8,128)(2,1)S(1)}, bf16[512,256]{0,1:T(8,128)(2,1)S(1)}, u32[]{:S(2)}, u32[]{:S(2)}) %collective-permute-start.3) | collective-permute-done | bytes 262176 | tf_op jit(solution)/shard_map/ppermute | solution.py:12
  71.3 0.0 collective-permute-start.4
  71.3 5.8 %collective-permute-done.4 = bf16[512,256]{0,1:T(8,128)(2,1)S(1)} collective-permute-done((bf16[512,256]{0,1:T(8,128)(2,1)S(1)}, bf16[512,256]{0,1:T(8,128)(2,1)S(1)}, u32[]{:S(2)}, u32[]{:S(2)}) %collective-permute-start.4) | collective-permute-done | bytes 262176 | tf_op jit(solution)/shard_map/ppermute | solution.py:12
  77.1 0.0 collective-permute-start.5
  77.1 16.7 %all-gather.5.cloned.1.call-done = bf16[1024,512]{1,0:T(8,128)(2,1)} async-done(((bf16[256,512]{1,0:T(8,128)(2,1)}), bf16[1024,512]{1,0:T(8,128)(2,1)}) %all-gather.5.cloned.1.call-update) | async-done | bytes 1048592 | tf_op jit(solution)/shard_map/all_gather | solution.py:47
  93.8 0.0 collective-permute-done.5
  93.8 5.0 %fusion.4 = f32[512,512]{0,1:T(8,128)S(1)} fusion(bf16[1024,512]{1,0:T(8,128)(2,1)} %all-gather.5.cloned.1.call-done, s32[]{:T(128)S(6)} %select_n.13, bf16[512,256]{0,1:T(8,128)(2,1)S(1)} %collective-permute-done.5, bf16[512,256]{0,1:T(8,128)(2,1)S(1)} %collective-permute-done.4, bf16[512,256]{0,1:T(8,128)(2,1)S(1)} %collective-permute-done.3, ...), kind=kOutput, calls=%fused_computation.20 | convolution fusion | flops 545259520 | bytes 3145732 | tf_op jit(solution)/shard_map/dot_general | solution.py:45
  98.9 1.3 %copy.9 = f32[512,2,256]{2,0,1:T(8,128)} copy(f32[512,2,256]{0,2,1:T(8,128)S(1)} %bitcast.36) | data formatting | bytes 2097152 | tf_op jit(solution)/shard_map/reshape | solution.py:51
  100.2 0.0 reduce-scatter.5.cloned.1.call-update
  100.2 20.0 %reduce-scatter.5.cloned.1.call-done = f32[512,1,256]{2,0,1:T(8,128)} async-done(((f32[512,2,256]{2,0,1:T(8,128)}), f32[512,1,256]{2,0,1:T(8,128)}) %reduce-scatter.5.cloned.1.call-update) | async-done | bytes 524304 | tf_op jit(solution)/shard_map/reduce_scatter | solution.py:50
  120.2 1.8 %convert_element_type.59 = bf16[512,1,256]{2,0,1:T(8,128)(2,1)} convert(f32[512,1,256]{2,0,1:T(8,128)} %reduce-scatter.5.cloned.1.call-done) | non-fusion elementwise | flops 131072 | bytes 786432 | tf_op jit(solution)/shard_map/convert_element_type | solution.py:72
  (5 shorter events, 0.1 us)
Async XLA Ops:
  6.5 33.6 %all-gather.3.cloned.1.call-start = ((), (), s32[]{:S(2)}) async-start(), calls=%async_computation.2 | async-start | bytes 1310720 | tf_op jit(solution)/shard_map/all_gather | solution.py:47
  7.4 2.0 %copy-start.3 = (s32[4,1,2]{0,2,1:T(2,128)S(1)}, s32[4,1,2]{0,2,1:T(2,128)}, u32[]{:S(2)}) copy-start(s32[4,1,2]{0,2,1:T(2,128)} %param.12) | copy-start | bytes 100
  7.6 2.2 %copy-start = (bf16[512,1,256]{2,0,1:T(8,128)(2,1)S(1)}, bf16[512,1,256]{2,0,1:T(8,128)(2,1)}, u32[]{:S(2)}) copy-start(bf16[512,1,256]{2,0,1:T(8,128)(2,1)} %param.9) | copy-start | bytes 786436
  9.4 54.8 %reduce-scatter.3.cloned.1.call-start = ((), (), s32[]{:S(2)}) async-start(), calls=%async_computation.3 | async-start | bytes 1572864 | tf_op jit(solution)/shard_map/reduce_scatter | solution.py:50
  9.8 6.5 %collective-permute-start = (bf16[512,256]{1,0:T(8,128)(2,1)S(1)}, bf16[512,256]{1,0:T(8,128)(2,1)S(1)}, u32[]{:S(2)}, u32[]{:S(2)}) collective-permute-start(bf16[512,256]{1,0:T(8,128)(2,1)S(1)} %bitcast_multiply_fusion.1), channel_id=1, source_target_pairs={{0,2},{2,4},{4,6},{6,0},{1,3},{3,5},{5,7},{7,1},{8,10},{10,12},{12... | collective-permute-start | bytes 786440 | tf_op jit(solution)/shard_map/ppermute | solution.py:12
  16.3 5.8 %collective-permute-start.1 = (bf16[512,256]{1,0:T(8,128)(2,1)S(1)}, bf16[512,256]{1,0:T(8,128)(2,1)S(1)}, u32[]{:S(2)}, u32[]{:S(2)}) collective-permute-start(bf16[512,256]{1,0:T(8,128)(2,1)S(1)} %collective-permute-done), channel_id=1, source_target_pairs={{0,2},{2,4},{4,6},{6,0},{1,3},{3,5},{5,7},{7,1},{8,10},{10,12},{12... | collective-permute-start | bytes 786440 | tf_op jit(solution)/shard_map/ppermute | solution.py:12
  22.1 5.8 %collective-permute-start.2 = (bf16[512,256]{1,0:T(8,128)(2,1)S(1)}, bf16[512,256]{1,0:T(8,128)(2,1)S(1)}, u32[]{:S(2)}, u32[]{:S(2)}) collective-permute-start(bf16[512,256]{1,0:T(8,128)(2,1)S(1)} %collective-permute-done.1), channel_id=1, source_target_pairs={{0,2},{2,4},{4,6},{6,0},{1,3},{3,5},{5,7},{7,1},{8,10},{10,12},{12... | collective-permute-start | bytes 786440 | tf_op jit(solution)/shard_map/ppermute | solution.py:12
  44.2 0.7 copy-start.2
  44.2 1.0 copy-start.1
  44.3 49.6 %all-gather.5.cloned.1.call-start = ((), (), s32[]{:S(2)}) async-start(), calls=%async_computation.4 | async-start | bytes 1310720 | tf_op jit(solution)/shard_map/all_gather | solution.py:47
  45.1 1.0 copy-start.4
  46.1 74.1 %reduce-scatter.5.cloned.1.call-start = ((), (), s32[]{:S(2)}) async-start(), calls=%async_computation.5 | async-start | bytes 1572864 | tf_op jit(solution)/shard_map/reduce_scatter | solution.py:50
  65.5 5.8 %collective-permute-start.3 = (bf16[512,256]{0,1:T(8,128)(2,1)S(1)}, bf16[512,256]{0,1:T(8,128)(2,1)S(1)}, u32[]{:S(2)}, u32[]{:S(2)}) collective-permute-start(bf16[512,256]{0,1:T(8,128)(2,1)S(1)} %bitcast_multiply_fusion), channel_id=1, source_target_pairs={{0,2},{2,4},{4,6},{6,0},{1,3},{3,5},{5,7},{7,1},{8,10},{10,12},{12... | collective-permute-start | bytes 786440 | tf_op jit(solution)/shard_map/ppermute | solution.py:12
  71.3 5.8 %collective-permute-start.4 = (bf16[512,256]{0,1:T(8,128)(2,1)S(1)}, bf16[512,256]{0,1:T(8,128)(2,1)S(1)}, u32[]{:S(2)}, u32[]{:S(2)}) collective-permute-start(bf16[512,256]{0,1:T(8,128)(2,1)S(1)} %collective-permute-done.3), channel_id=1, source_target_pairs={{0,2},{2,4},{4,6},{6,0},{1,3},{3,5},{5,7},{7,1},{8,10},{10,12},{12... | collective-permute-start | bytes 786440 | tf_op jit(solution)/shard_map/ppermute | solution.py:12
  77.1 16.7 %collective-permute-start.5 = (bf16[512,256]{0,1:T(8,128)(2,1)S(1)}, bf16[512,256]{0,1:T(8,128)(2,1)S(1)}, u32[]{:S(2)}, u32[]{:S(2)}) collective-permute-start(bf16[512,256]{0,1:T(8,128)(2,1)S(1)} %collective-permute-done.4), channel_id=1, source_target_pairs={{0,2},{2,4},{4,6},{6,0},{1,3},{3,5},{5,7},{7,1},{8,10},{10,12},{12... | collective-permute-start | bytes 786440 | tf_op jit(solution)/shard_map/ppermute | solution.py:12
Sparse Core Ops, SparseCore 0:
  9.5 30.6 all-gather.2
  44.4 19.7 reduce-scatter.2
  65.9 27.9 all-gather.4
  100.3 19.7 reduce-scatter.4
